TPU v7x, 256 devices: a whole 4x4x8 slice. The times are simulated.
256 devices in a mesh: gx: 8 (over z_lo, y), gy: 4 (over x), gz: 8 (over z_hi, core).
Axes of the slice: x: 4, y: 4, z: 8 (z_hi: 4, z_lo: 2; z = z_hi * 2 + z_lo), core: 2. Of those that a mesh axis runs over, the one named last changes fastest.
Arguments:
- coordinates: float32 [8, 4, 8, 3, 16, 128], P('gx', 'gy', 'gz'), may hold values from -8 to 168
- neighbours: int32 [8, 4, 8, 16, 128], P('gx', 'gy', 'gz'), may hold values from 0 to 991, as said below
- pair_index: int32 [8, 4, 8, 4, 15360], P('gx', 'gy', 'gz'), may hold values from 0 to 127, as said below
- pair_live: int32 [8, 4, 8, 15360], P('gx', 'gy', 'gz'), may hold values 0 or 1
- basis: bfloat16 [8, 4, 8, 128, 1536], P('gx', 'gy', 'gz'), may hold values from -50 to 50
Outputs:
- next_basis: float32 [8, 4, 8, 128, 1536], P('gx', 'gy', 'gz')
- ritz_matrix: float32 [256, 256], replicated
Inputs may be any that keep to these rules, and one draw needn't show every extreme that they name: neighbours[x, y, z, 0, f] = 864 + f. Any other entry c < 864 names frame c % 32 of the domain offset by (c // 32 // 9 - 1, c // 32 // 3 % 3 - 1, c // 32 % 3 - 1), which lies in the grid and is not the domain itself; an entry c >= 864 names the domain's own frame c - 864, never the row's frame f. `pair_index`: row 0 holds a frame f < 128, row 1 a slot 1 to 15, rows 2 and 3 atoms below 16.
All inputs are finite; a program needn't handle non-finite values. No bound on the sum of `pair_live` on one device may be relied on, other than what follows from the above.
Results may differ from a plain program's by a relative error of at most 0.0003.
Values may be sent and summed in bfloat16 or wider, within the bound.
A program may use at most 128 MiB of HBM per device.

v0:
```python
import jax
import jax.numpy as jnp
from jax import lax
from jax.sharding import Mesh
from jax.sharding import PartitionSpec as P

GX = ("gx_0", "gx_1")
GZ = ("gz_0", "gz_1")
stiffness = 0.01


def padded(cells, sides, width, closed):
    for axis, dim in sides:
        count = lax.axis_size(axis)
        ends = count if closed else count - 1
        head = lax.slice_in_dim(cells, 0, width, axis=dim)
        tail = lax.slice_in_dim(cells, cells.shape[dim] - width, cells.shape[dim], axis=dim)
        cells = jnp.concatenate(
            [
                lax.ppermute(tail, axis, [(i, (i + 1) % count) for i in range(ends)]),
                cells,
                lax.ppermute(head, axis, [((i + 1) % count, i) for i in range(ends)]),
            ],
            axis=dim,
        )
    return cells


def rows_for(lines, size):
    spare = -len(lines) % size
    return jnp.pad(lines, [(0, spare)] + [(0, 0)] * (lines.ndim - 1))


def sum_in_two_steps(x, near, far):
    lines = x.reshape(-1, *x.shape[1:][-1:])
    padded = rows_for(lines, lax.axis_size(near))
    own = lax.psum_scatter(padded, near, scatter_dimension=0, tiled=True)
    own = lax.psum(own, far)
    whole = lax.all_gather(own, near, axis=0, tiled=True)
    return whole[: len(lines)].reshape(x.shape)


def cross_product(left, right):
    return jnp.stack(
        [
            left[1] * right[2] - left[2] * right[1],
            left[2] * right[0] - left[0] * right[2],
            left[0] * right[1] - left[1] * right[0],
        ]
    )


def assemble(visible, neighbours, pair_index, pair_live):
    columns = visible.shape[2]
    frames = neighbours.shape[1]
    slots = neighbours.shape[0]
    centres = jnp.mean(visible, axis=1)
    own_frame = pair_index[0]
    slot_of = pair_index[1]
    atom_a = pair_index[2]
    atom_b = pair_index[3]
    self_column = own_frame + (columns - frames)
    partner = jnp.take(neighbours.reshape(-1), slot_of * frames + own_frame, axis=0)
    flat_coords = visible.reshape(3, -1)
    pos_a = jnp.take(flat_coords, atom_a * columns + self_column, axis=1)
    pos_b = jnp.take(flat_coords, atom_b * columns + partner, axis=1)
    arm_a = pos_a - jnp.take(centres, self_column, axis=1)
    arm_b = pos_b - jnp.take(centres, partner, axis=1)
    spring = pos_a - pos_b
    length_sq = jnp.maximum(jnp.sum(spring * spring, axis=0), 1.0)
    weight = stiffness * pair_live.astype(jnp.float32) / length_sq
    left_vec = jnp.concatenate([spring, cross_product(arm_a, spring)], axis=0)
    right_vec = jnp.concatenate([spring, cross_product(arm_b, spring)], axis=0)
    off_terms = -(weight * left_vec)[:, None, :] * right_vec[None, :, :]
    self_terms = (weight * left_vec)[:, None, :] * left_vec[None, :, :]
    values = jnp.concatenate([off_terms.reshape(36, -1).T, self_terms.reshape(36, -1).T], axis=0)
    row_keys = jnp.concatenate([slot_of * frames + own_frame, own_frame], axis=0)
    blocks = jnp.zeros((slots * frames, 36), jnp.float32).at[row_keys].add(values)
    return blocks.reshape(slots, frames, 36)


def apply_blocks(blocks, neighbours, vector_table):
    frames = neighbours.shape[1]
    vector_count = vector_table.shape[1] // 6

    def add_slot(slot_index, totals):
        gathered = jnp.take(vector_table, neighbours[slot_index], axis=0)
        coeffs = blocks[slot_index]
        pieces = [
            gathered[:, inner_dof * vector_count : (inner_dof + 1) * vector_count]
            for inner_dof in range(6)
        ]
        updated = []
        for outer_dof in range(6):
            total = totals[outer_dof]
            for inner_dof in range(6):
                column = coeffs[:, 6 * outer_dof + inner_dof : 6 * outer_dof + inner_dof + 1]
                total = total + column * pieces[inner_dof].astype(jnp.float32)
            updated.append(total)
        return tuple(updated)

    start = tuple((jnp.zeros((frames, vector_count), jnp.float32) for outer_dof in range(6)))
    totals = lax.fori_loop(0, neighbours.shape[0], add_slot, start)
    return jnp.concatenate(totals, axis=1)


def gram_matrix(left, right):
    return lax.dot_general(
        left, right, (((0,), (0,)), ((), ())), preferred_element_type=jnp.float32
    )


def rayleigh_ritz(basis_gram, cross_gram, image_gram, image_rows, total_rows):
    factor = jnp.linalg.cholesky(basis_gram / total_rows)
    sym_cross = (cross_gram + cross_gram.T) / (2.0 * total_rows)
    half_solved = lax.linalg.triangular_solve(factor, sym_cross, left_side=True, lower=True)
    ritz_matrix = lax.linalg.triangular_solve(factor, half_solved.T, left_side=True, lower=True)
    image_factor = jnp.linalg.cholesky(image_gram / total_rows)
    next_rows = lax.linalg.triangular_solve(
        image_factor, image_rows, left_side=False, lower=True, transpose_a=True
    )
    return (ritz_matrix, next_rows)


def per_device(coordinates, neighbours, pair_index, pair_live, basis):
    frames = basis.shape[3]
    vector_count = basis.shape[4] // 6
    rim_frames = frames // 4
    atoms_per = coordinates.shape[4]
    total_rows = 6 * frames * lax.axis_size(GX) * lax.axis_size("gy") * lax.axis_size(GZ)
    own_basis = basis[0, 0, 0]
    own_lists = neighbours[0, 0, 0]
    flat_basis = own_basis.reshape(frames * 6, vector_count)
    basis_local = gram_matrix(flat_basis, flat_basis)
    near_coords = padded(
        coordinates[:, :, :, :, :, :rim_frames], ((GX, 0), ("gy", 1), (GZ, 2)), 1, False
    )
    rim_rows = basis[:, :, :, :rim_frames, :]
    near_basis = padded(rim_rows, ((GX, 0), ("gy", 1), (GZ, 2)), 1, False)
    ghost_coords = (
        near_coords.reshape(27, 3, atoms_per, rim_frames)
        .transpose(1, 2, 0, 3)
        .reshape(3, atoms_per, 27 * rim_frames)
    )
    visible = jnp.concatenate([ghost_coords, coordinates[0, 0, 0]], axis=2)
    blocks = assemble(visible, own_lists, pair_index[0, 0, 0], pair_live[0, 0, 0])
    vector_table = jnp.concatenate(
        [near_basis.reshape(27 * rim_frames, 6 * vector_count), own_basis], axis=0
    )
    image_rows = apply_blocks(blocks, own_lists, vector_table)
    rounded = image_rows.astype(jnp.bfloat16).reshape(frames * 6, vector_count)
    cross_local = gram_matrix(flat_basis, rounded)
    image_local = gram_matrix(rounded, rounded)
    basis_gram, cross_gram, image_gram = (
        sum_in_two_steps(basis_local, "gz_1", ("gx_0", "gx_1", "gy", "gz_0")),
        sum_in_two_steps(cross_local, "gz_1", ("gx_0", "gx_1", "gy", "gz_0")),
        sum_in_two_steps(image_local, "gz_1", ("gx_0", "gx_1", "gy", "gz_0")),
    )
    ritz_matrix, next_rows = rayleigh_ritz(
        basis_gram, cross_gram, image_gram, image_rows.reshape(frames * 6, vector_count), total_rows
    )
    next_basis = next_rows.reshape(1, 1, 1, frames, 6 * vector_count)
    return (next_basis, ritz_matrix)


def solution(mesh):
    torus = Mesh(
        mesh.devices.reshape(2, 4, mesh.shape["gy"], 4, 2), ("gx_0", "gx_1", "gy", "gz_0", "gz_1")
    )
    in_specs = (
        P(GX, "gy", GZ, None, None, None),
        P(GX, "gy", GZ, None, None),
        P(GX, "gy", GZ, None, None),
        P(GX, "gy", GZ, None),
        P(GX, "gy", GZ, None, None),
    )
    out_specs = (P(GX, "gy", GZ, None, None), P())
    return jax.shard_map(
        per_device, mesh=torus, in_specs=in_specs, out_specs=out_specs, check_vma=False
    )
```

profile of v0, /device:TPU:1, one launch (start us, length us, event | category | flops | bytes accessed | tf_op | source)
XLA Modules:
  0.0 1204.4 jit_solution(14516050575677457552)
XLA Ops:
  7.2 4.0 collective-permute-start
  13.5 4.0 collective-permute-start.6
  24.2 84.9 %gather_fusion.1 = s32[15360]{0:T(1024)S(1)} fusion(s32[2048]{0:T(1024)S(1)} %bitcast.221, s32[15360]{0:T(1024)S(1)} %broadcast_clamp_fusion), kind=kCustom, calls=%fused_computation.5 | custom fusion | bytes 184320 | tf_op jit(solution)/shard_map/jit(_take)/gather | solution.py:63
  118.4 7.7 collective-permute-start.4
  129.0 5.3 collective-permute-done.5
  134.9 4.6 copy.145
  139.6 54.4 %gather_fusion.3 = f32[15360,3]{1,0:T(8,128)} fusion(f32[3,15872]{0,1:T(8,128)} %bitcast.223, s32[15360]{0:T(1024)S(1)} %get-tuple-element.414), kind=kCustom, calls=%fused_computation.3.clone | custom fusion | bytes 430080 | tf_op jit(solution)/shard_map/jit(_take)/gather | solution.py:66
  194.0 5.0 copy.147
  199.3 51.1 %gather_fusion.5 = f32[15360,3]{1,0:T(8,128)} fusion(f32[3,992]{0,1:T(8,128)S(1)} %broadcast_multiply_fusion.2, s32[15360]{0:T(1024)S(1)} %get-tuple-element.413), kind=kCustom, calls=%fused_computation.4.clone | custom fusion | bytes 430080 | tf_op jit(solution)/shard_map/jit(_take)/gather | solution.py:68
  250.4 5.0 copy.150
  255.4 54.4 %gather_fusion.2 = f32[15360,3]{1,0:T(8,128)} fusion(f32[3,15872]{0,1:T(8,128)} %bitcast.224, s32[15360]{0:T(1024)S(1)} %get-tuple-element.418), kind=kCustom, calls=%fused_computation.clone | custom fusion | bytes 430080 | tf_op jit(solution)/shard_map/jit(_take)/gather | solution.py:65
  309.9 5.0 copy.146
  314.9 51.1 %gather_fusion.4 = f32[15360,3]{1,0:T(8,128)} fusion(f32[3,992]{0,1:T(8,128)S(1)} %broadcast_multiply_fusion.2, s32[15360]{0:T(1024)S(1)} %get-tuple-element.417), kind=kCustom, calls=%fused_computation.1.clone | custom fusion | bytes 430080 | tf_op jit(solution)/shard_map/jit(_take)/gather | solution.py:67
  366.1 5.0 copy.149
  392.9 4.2 pad_maximum_fusion
  397.1 10.4 copy.151
  407.5 163.6 %scatter_custom_fusion = f32[2048,36]{1,0:T(8,128)S(1)} fusion(s32[30720]{0:T(1024)} %bitcast.248, f32[30720,36]{1,0:T(8,128)} %copy.151, f32[]{:T(128)} %constant.163.clone.1), kind=kCustom, calls=%fused_computation.145 | custom fusion | flops 1105920 | bytes 295424 | tf_op jit(solution)/shard_map/scatter-add | solution.py:78
  574.2 217.5 %while.30 = (s32[]{:T(128)}, f32[128,256]{1,0:T(8,128)}, f32[128,256]{1,0:T(8,128)}, f32[128,256]{1,0:T(8,128)}, f32[128,256]{1,0:T(8,128)}, /*index=5*/f32[128,...) while((s32[]{:T(128)}, f32[128,256]{1,0:T(8,128)}, ...), condition=%wide.region_4.7_spmd.clone, body=%wide.region_3.6_spmd.clone.sunk | while | flops 3934339 | bytes 5604240 | solution.py:103
  799.9 21.3 %reduce-scatter.8.cloned.1.call-done = f32[128,256]{0,1:T(8,128)} async-done(((f32[256,256]{0,1:T(8,128)}), f32[128,256]{0,1:T(8,128)}) %reduce-scatter.8.cloned.1.call-update) | async-done | bytes 131088 | tf_op jit(solution)/shard_map/reduce_scatter | solution.py:37
  821.2 17.4 %reduce-scatter.4.cloned.1.call-done = f32[128,256]{0,1:T(8,128)} async-done(((f32[256,256]{0,1:T(8,128)}), f32[128,256]{0,1:T(8,128)}) %reduce-scatter.4.cloned.1.call-update) | async-done | bytes 131088 | tf_op jit(solution)/shard_map/reduce_scatter | solution.py:37
  838.8 219.5 %all-reduce.4.cloned.1.call-done = (f32[128,256]{0,1:T(8,128)}, f32[128,256]{0,1:T(8,128)}, f32[128,256]{0,1:T(8,128)}) async-done(((f32[128,256]{0,1:T(8,128)}, f32[128,256]{0,1:T(8,128)}, f32[128,256]{0,1:T(8,128)}), (f32[128,256]{0,1:T(8,128)}, f32[128,256]{0,1:T(8,128)}, f32[128,256]{0,1:T(8,128)})) %all-reduce.4.cloned.1.call-update) | async-done | bytes 393232 | tf_op jit(solution)/shard_map/psum | solution.py:38
  1058.3 7.3 all_gather.10
  1065.9 11.7 cholesky.164
  1077.7 9.8 custom-call.24
  1088.0 11.7 cholesky.181
  1102.5 4.3 while.31
  1106.9 19.7 %custom-call.26 = f32[2,128,128]{1,2,0:T(8,128)S(1)} custom-call(f32[2,128,128]{2,1,0:T(8,128)S(1)} %get-tuple-element.242), custom_call_target="InvertDiagBlocksLowerTriangular" | custom-call | tf_op jit(solution)/shard_map/triangular_solve/custom-call.4 | solution.py:117
  1133.8 11.7 cholesky.130
  1145.5 9.8 custom-call.23
  1155.8 11.7 cholesky.147
  1170.3 4.2 while.29
  1174.5 19.7 %custom-call.14 = f32[2,128,128]{1,2,0:T(8,128)S(1)} custom-call(f32[2,128,128]{2,1,0:T(8,128)S(1)} %get-tuple-element.201), custom_call_target="InvertDiagBlocksLowerTriangular" | custom-call | tf_op jit(solution)/shard_map/triangular_solve | solution.py:119
  (386 shorter events, 294.4 us)
Async XLA Ops:
  7.2 17.0 %copy-start.11 = (s32[1,1,1,15360]{3,2,1,0:T(1,128)S(1)}, s32[1,1,1,15360]{3,2,1,0:T(1,128)}, u32[]{:S(2)}) copy-start(s32[1,1,1,15360]{3,2,1,0:T(1,128)} %param.17) | copy-start | bytes 184324
  7.2 17.0 %copy-start = (s32[1,1,1,16,128]{4,3,2,1,0:T(8,128)S(1)}, s32[1,1,1,16,128]{4,3,2,1,0:T(8,128)}, u32[]{:S(2)}) copy-start(s32[1,1,1,16,128]{4,3,2,1,0:T(8,128)} %param.15) | copy-start | bytes 24580
  7.2 792.7 %reduce-scatter.6.cloned.1.call-start = ((), (), s32[]{:S(2)}) async-start(), calls=%async_computation.4 | async-start | bytes 393216 | tf_op jit(solution)/shard_map/reduce_scatter | solution.py:37
  7.2 102.8 %collective-permute-start = (f32[1,1,1,3,16,32]{5,4,3,2,1,0:T(8,128)}, f32[1,1,1,3,16,32]{5,4,3,2,1,0:T(8,128)S(1)}, u32[]{:S(2)}, u32[]{:S(2)}) collective-permute-start(f32[1,1,1,3,16,32]{5,4,3,2,1,0:T(8,128)} %bitcast.240), channel_id=1, source_target_pairs={{0,32},{32,64},{64,96},{96,128},{128,160},{160,192},{192,224},{1,3... | collective-permute-start | bytes 18440 | tf_op jit(solution)/shard_map/ppermute | solution.py:20
  11.3 98.8 %collective-permute-start.1 = (f32[1,1,1,3,16,32]{5,4,3,2,1,0:T(8,128)}, f32[1,1,1,3,16,32]{5,4,3,2,1,0:T(8,128)S(1)}, u32[]{:S(2)}, u32[]{:S(2)}) collective-permute-start(f32[1,1,1,3,16,32]{5,4,3,2,1,0:T(8,128)} %bitcast.241), channel_id=1, source_target_pairs={{32,0},{64,32},{96,64},{128,96},{160,128},{192,160},{224,192},{33,... | collective-permute-start | bytes 18440 | tf_op jit(solution)/shard_map/ppermute | solution.py:22
  13.5 359.4 %collective-permute-start.6 = (bf16[1,1,1,32,1536]{4,3,2,1,0:T(8,128)(2,1)S(1)}, bf16[1,1,1,32,1536]{4,3,2,1,0:T(8,128)(2,1)S(1)}, u32[]{:S(2)}, u32[]{:S(2)}) collective-permute-start(bf16[1,1,1,32,1536]{4,3,2,1,0:T(8,128)(2,1)S(1)} %slice.420), channel_id=1, source_target_pairs={{0,32},{32,64},{64,96},{96,128},{128,160},{160,192},{192,224},{1,3... | collective-permute-start | bytes 294920 | tf_op jit(solution)/shard_map/ppermute | solution.py:20
  17.5 355.4 %collective-permute-start.7 = (bf16[1,1,1,32,1536]{4,3,2,1,0:T(8,128)(2,1)S(1)}, bf16[1,1,1,32,1536]{4,3,2,1,0:T(8,128)(2,1)S(1)}, u32[]{:S(2)}, u32[]{:S(2)}) collective-permute-start(bf16[1,1,1,32,1536]{4,3,2,1,0:T(8,128)(2,1)S(1)} %slice.420), channel_id=1, source_target_pairs={{32,0},{64,32},{96,64},{128,96},{160,128},{192,160},{224,192},{33,... | collective-permute-start | bytes 294920 | tf_op jit(solution)/shard_map/ppermute | solution.py:22
  20.1 89.1 %copy-start.2 = (bf16[768,256]{1,0:T(8,128)(2,1)}, bf16[768,256]{1,0:T(8,128)(2,1)S(1)}, u32[]{:S(2)}) copy-start(bf16[768,256]{1,0:T(8,128)(2,1)S(1)} %reshape_squeeze.7) | copy-start | bytes 1179652
  21.1 800.0 %reduce-scatter.8.cloned.1.call-start = ((), (), s32[]{:S(2)}) async-start(), calls=%async_computation.5 | async-start | bytes 393216 | tf_op jit(solution)/shard_map/reduce_scatter | solution.py:37
  24.2 85.9 %copy-start.8 = (f32[1,1,1,3,16,128]{5,4,3,2,1,0:T(8,128)S(1)}, f32[1,1,1,3,16,128]{5,4,3,2,1,0:T(8,128)}, u32[]{:S(2)}) copy-start(f32[1,1,1,3,16,128]{5,4,3,2,1,0:T(8,128)} %param.14) | copy-start | bytes 73732
  110.1 4.5 collective-permute-start.2
  113.2 5.1 collective-permute-start.3
  118.4 10.6 collective-permute-start.4
  126.1 8.2 collective-permute-start.5
  372.9 12.2 %copy-start.6 = (bf16[1,1,1,32,1536]{4,3,2,1,0:T(8,128)(2,1)}, bf16[1,1,1,32,1536]{4,3,2,1,0:T(8,128)(2,1)S(1)}, u32[]{:S(2)}) copy-start(bf16[1,1,1,32,1536]{4,3,2,1,0:T(8,128)(2,1)S(1)} %collective-permute-done.7) | copy-start | bytes 294916
  373.6 11.4 collective-permute-start.8
  376.8 8.3 collective-permute-start.9
  381.6 11.3 copy-start.1
  385.0 12.1 %copy-start.5 = (bf16[3,1,1,32,1536]{4,3,2,1,0:T(8,128)(2,1)}, bf16[3,1,1,32,1536]{4,3,2,1,0:T(8,128)(2,1)S(1)}, u32[]{:S(2)}) copy-start(bf16[3,1,1,32,1536]{4,3,2,1,0:T(8,128)(2,1)S(1)} %collective-permute-done.8) | copy-start | bytes 884740
  387.2 185.0 %collective-permute-start.10 = (bf16[3,3,1,32,1536]{4,3,2,1,0:T(8,128)(2,1)}, bf16[3,3,1,32,1536]{4,3,2,1,0:T(8,128)(2,1)}, u32[]{:S(2)}, u32[]{:S(2)}) collective-permute-start(bf16[3,3,1,32,1536]{4,3,2,1,0:T(8,128)(2,1)} %pad_maximum_fusion.3), channel_id=1, source_target_pairs={{0,1},{1,2},{2,3},{3,4},{4,5},{5,6},{6,7},{8,9},{9,10},{10,11},{11... | collective-permute-start | bytes 2654216 | tf_op jit(solution)/shard_map/ppermute | solution.py:20
  389.7 182.5 %collective-permute-start.11 = (bf16[3,3,1,32,1536]{4,3,2,1,0:T(8,128)(2,1)}, bf16[3,3,1,32,1536]{4,3,2,1,0:T(8,128)(2,1)}, u32[]{:S(2)}, u32[]{:S(2)}) collective-permute-start(bf16[3,3,1,32,1536]{4,3,2,1,0:T(8,128)(2,1)} %pad_maximum_fusion.3), channel_id=1, source_target_pairs={{1,0},{2,1},{3,2},{4,3},{5,4},{6,5},{7,6},{9,8},{10,9},{11,10},{12... | collective-permute-start | bytes 2654216 | tf_op jit(solution)/shard_map/ppermute | solution.py:22
  397.1 175.1 %copy-start.7 = (bf16[1,1,1,32,1536]{4,3,2,1,0:T(8,128)(2,1)S(1)}, bf16[1,1,1,32,1536]{4,3,2,1,0:T(8,128)(2,1)}, u32[]{:S(2)}) copy-start(bf16[1,1,1,32,1536]{4,3,2,1,0:T(8,128)(2,1)} %copy-done.6) | copy-start | bytes 294916
  571.1 2.9 copy-start.4
  791.7 6.0 copy-start.3
  798.8 39.8 %reduce-scatter.4.cloned.1.call-start = ((), (), s32[]{:S(2)}) async-start(), calls=%async_computation.3 | async-start | bytes 393216 | tf_op jit(solution)/shard_map/reduce_scatter | solution.py:37
  799.8 258.5 %all-reduce.4.cloned.1.call-start = ((), (), s32[]{:S(2)}) async-start(), calls=%async_computation.6 | async-start | bytes 786432 | tf_op jit(solution)/shard_map/psum | solution.py:38
  1058.3 68.2 %copy-start.10 = (f32[128,256]{0,1:T(8,128)S(1)}, f32[128,256]{0,1:T(8,128)}, u32[]{:S(2)}) copy-start(f32[128,256]{0,1:T(8,128)} %get-tuple-element.340) | copy-start | bytes 393220
  1102.4 29.1 %copy-start.9 = (f32[128,256]{0,1:T(8,128)S(1)}, f32[128,256]{0,1:T(8,128)}, u32[]{:S(2)}) copy-start(f32[128,256]{0,1:T(8,128)} %get-tuple-element.339) | copy-start | bytes 393220
Sparse Core Ops, SparseCore 0:
  21.3 19.8 reduce-scatter.5
  798.9 22.2 reduce-scatter.7
  824.2 14.3 reduce-scatter.3
  844.2 214.0 all-reduce.3
where the time goes:
time: 1220 us; the launch traced here: 1200 us
  other arithmetic  469 us (38%)
  local copies, waits for them, and re-layouts  395 us (32%)
  waiting for transfers between devices  268 us (22%)
  starting transfers between devices  35 us (3%)
  between operations  17.6 us (1%)
    psum x1, waiting for transfers between devices, sum_in_two_steps(): own = lax.psum(own, far)  220 us
    scatter-add x1, other arithmetic, assemble(): jnp.zeros((slots * frames, 36), jnp.float32).at[row_keys].add(values)  164 us
    add x96, other arithmetic, add_slot(): total = total + column * pieces[inner_dof].astype(jnp.float32)  161 us
    gather x1, local copies, waits for them, and re-layouts, assemble(): jnp.take(neighbours.reshape(-1), slot_of * frames + own_frame, axis=0)  84.9 us
    gather x2, local copies, waits for them, and re-layouts, assemble(): pos_a = jnp.take(flat_coords, atom_a * columns + self_column, axis=1)  59.5 us
    gather x2, local copies, waits for them, and re-layouts, assemble(): pos_b = jnp.take(flat_coords, atom_b * columns + partner, axis=1)  59.4 us
    gather x2, local copies, waits for them, and re-layouts, assemble(): arm_a = pos_a - jnp.take(centres, self_column, axis=1)  56.2 us
    gather x2, local copies, waits for them, and re-layouts, assemble(): arm_b = pos_b - jnp.take(centres, partner, axis=1)  56.2 us
  transfers between devices with their start and end apart: 16, of which 6 were waited for; matrix products, arithmetic and copies ran while one was open for 62% of the time, Pallas kernels for 0%

commit v1 on v0

--- a/solution.py
+++ b/solution.py
@@ -3,6 +3,7 @@
 from jax import lax
 from jax.sharding import Mesh
 from jax.sharding import PartitionSpec as P
+from jax.lax import all_gather
 
 GX = ("gx_0", "gx_1")
 GZ = ("gz_0", "gz_1")
@@ -35,7 +36,7 @@
     lines = x.reshape(-1, *x.shape[1:][-1:])
     padded = rows_for(lines, lax.axis_size(near))
     own = lax.psum_scatter(padded, near, scatter_dimension=0, tiled=True)
-    own = lax.psum(own, far)
+    own = all_gather(own, far).sum(axis=0)
     whole = lax.all_gather(own, near, axis=0, tiled=True)
     return whole[: len(lines)].reshape(x.shape)
 

time: 1220 us -> 3230 us (2.65)
  waiting for transfers between devices: 268 us -> 1980 us
  blocking collectives: 11.3 us -> 297 us
    all_gather x0 -> x3, waiting for transfers between devices: none -> 1940 us  [sum_in_two_steps(): own = all_gather(own, far).sum(axis=0)]
    all_gather x3, blocking collectives: 11.3 us -> 297 us  [sum_in_two_steps(): whole = lax.all_gather(own, near, axis=0, tiled=True)]
    psum x1 -> x0, waiting for transfers between devices: 220 us -> none  [sum_in_two_steps(): own = lax.psum(own, far)]
  transfers between devices with their start and end apart: 16 -> 18, of which waited for: 6 -> 8; matrix products, arithmetic and copies ran while one was open for 62% -> 27% of each run, Pallas kernels for 0% -> 0%
where the time goes in v1:
time: 3230 us; the launch traced here: 3210 us
  waiting for transfers between devices  1980 us (61%)
  other arithmetic  475 us (15%)
  local copies, waits for them, and re-layouts  396 us (12%)
  blocking collectives  297 us (9%)
  starting transfers between devices  40.8 us (1%)
    all_gather x3, waiting for transfers between devices, sum_in_two_steps(): own = all_gather(own, far).sum(axis=0)  1940 us
    all_gather x3, blocking collectives, sum_in_two_steps(): whole = lax.all_gather(own, near, axis=0, tiled=True)  297 us
    scatter-add x1, other arithmetic, assemble(): jnp.zeros((slots * frames, 36), jnp.float32).at[row_keys].add(values)  164 us
    add x96, other arithmetic, add_slot(): total = total + column * pieces[inner_dof].astype(jnp.float32)  161 us
    gather x1, local copies, waits for them, and re-layouts, assemble(): jnp.take(neighbours.reshape(-1), slot_of * frames + own_frame, axis=0)  84.9 us
  transfers between devices with their start and end apart: 18, of which 8 were waited for; matrix products, arithmetic and copies ran while one was open for 27% of the time, Pallas kernels for 0%

profile of v1, /device:TPU:1, one launch (start us, length us, event | category | flops | bytes accessed | tf_op | source)
XLA Modules:
  0.0 3213.3 jit_solution(8397292651530636338)
XLA Ops:
  26.4 84.9 %gather_fusion.1 = s32[15360]{0:T(1024)S(1)} fusion(s32[2048]{0:T(1024)S(1)} %bitcast.228, s32[15360]{0:T(1024)S(1)} %broadcast_clamp_fusion), kind=kCustom, calls=%fused_computation.5 | custom fusion | bytes 184320 | tf_op jit(solution)/shard_map/jit(_take)/gather | solution.py:64
  118.2 6.7 collective-permute-start.5
  136.2 54.4 %gather_fusion.3 = f32[15360,3]{1,0:T(8,128)} fusion(f32[3,15872]{0,1:T(8,128)} %bitcast.230, s32[15360]{0:T(1024)S(1)} %get-tuple-element.411), kind=kCustom, calls=%fused_computation.3.clone | custom fusion | bytes 430080 | tf_op jit(solution)/shard_map/jit(_take)/gather | solution.py:67
  190.6 5.0 copy.137
  195.6 54.4 %gather_fusion.2 = f32[15360,3]{1,0:T(8,128)} fusion(f32[3,15872]{0,1:T(8,128)} %bitcast.231, s32[15360]{0:T(1024)S(1)} %get-tuple-element.415), kind=kCustom, calls=%fused_computation.clone | custom fusion | bytes 430080 | tf_op jit(solution)/shard_map/jit(_take)/gather | solution.py:66
  255.4 51.1 %gather_fusion.5 = f32[15360,3]{1,0:T(8,128)} fusion(f32[3,992]{0,1:T(8,128)S(1)} %broadcast_multiply_fusion.2, s32[15360]{0:T(1024)S(1)} %get-tuple-element.410), kind=kCustom, calls=%fused_computation.4.clone | custom fusion | bytes 430080 | tf_op jit(solution)/shard_map/jit(_take)/gather | solution.py:69
  311.5 51.1 %gather_fusion.4 = f32[15360,3]{1,0:T(8,128)} fusion(f32[3,992]{0,1:T(8,128)S(1)} %broadcast_multiply_fusion.2, s32[15360]{0:T(1024)S(1)} %get-tuple-element.414), kind=kCustom, calls=%fused_computation.1.clone | custom fusion | bytes 430080 | tf_op jit(solution)/shard_map/jit(_take)/gather | solution.py:68
  371.4 5.3 collective-permute-start.8
  387.8 5.7 collective-permute-start.10
  397.8 10.3 copy.141
  408.1 163.6 %scatter_custom_fusion = f32[2048,36]{1,0:T(8,128)S(1)} fusion(s32[30720]{0:T(1024)} %bitcast.258, f32[30720,36]{1,0:T(8,128)} %copy.141, f32[]{:T(128)} %constant.163.clone.1), kind=kCustom, calls=%fused_computation.146 | custom fusion | flops 1105920 | bytes 295424 | tf_op jit(solution)/shard_map/scatter-add | solution.py:79
  574.9 190.0 %while.30 = (s32[]{:T(128)}, f32[128,256]{1,0:T(8,128)}, f32[128,256]{1,0:T(8,128)}, f32[128,256]{1,0:T(8,128)}, f32[128,256]{1,0:T(8,128)}, /*index=5*/f32[128,...) while((s32[]{:T(128)}, f32[128,256]{1,0:T(8,128)}, ...), condition=%wide.region_4.7_spmd.clone, body=%wide.region_3.6_spmd.clone.sunk | while | flops 3934339 | bytes 5604248 | solution.py:104
  773.6 17.2 reduce-scatter.4.cloned.1.call-done
  790.9 17.3 reduce-scatter.8.cloned.1.call-done
  808.5 613.7 %all-gather.9.cloned.1.call-done = f32[16384,256]{1,0:T(8,128)} async-done(((f32[128,256]{1,0:T(8,128)}), f32[16384,256]{1,0:T(8,128)}) %all-gather.9.cloned.1.call-update) | async-done | bytes 16777232 | tf_op jit(solution)/shard_map/all_gather | solution.py:39
  1422.2 6.8 reduce_sum.48
  1429.1 92.9 %all_gather.32 = f32[256,256]{0,1:T(8,128)S(1)} all-gather(f32[128,256]{0,1:T(8,128)S(1)} %copy.147), channel_id=1, replica_groups=mesh['gx_0'=2,'gx_1'=4,'gy'=4,'gz_0'=4,'gz_1'=2] {'gz_1'}, dimensions={0}, use_global_device_ids=true | all-gather | bytes 393216 | tf_op jit(solution)/shard_map/all_gather | solution.py:40
  1522.3 11.7 cholesky.164
  1534.1 9.8 custom-call.24
  1544.3 11.7 cholesky.181
  1562.0 19.7 custom-call.26
  1581.6 635.5 %all-gather.7.cloned.1.call-done = f32[16384,256]{1,0:T(8,128)} async-done(((f32[128,256]{1,0:T(8,128)}), f32[16384,256]{1,0:T(8,128)}) %all-gather.7.cloned.1.call-update) | async-done | bytes 16777232 | tf_op jit(solution)/shard_map/all_gather | solution.py:39
  2217.1 6.8 reduce_sum.47
  2224.0 87.6 %all_gather.29 = f32[256,256]{0,1:T(8,128)S(1)} all-gather(f32[128,256]{0,1:T(8,128)S(1)} %copy.144), channel_id=1, replica_groups=mesh['gx_0'=2,'gx_1'=4,'gy'=4,'gz_0'=4,'gz_1'=2] {'gz_1'}, dimensions={0}, use_global_device_ids=true | all-gather | bytes 393216 | tf_op jit(solution)/shard_map/all_gather | solution.py:40
  2311.8 11.7 cholesky.130
  2323.6 9.8 custom-call.23
  2333.9 11.7 cholesky.147
  2352.4 19.7 custom-call.14
  2375.4 689.5 %all-gather.11.cloned.1.call-done = f32[16384,256]{0,1:T(8,128)} async-done(((f32[128,256]{0,1:T(8,128)}), f32[16384,256]{0,1:T(8,128)}) %all-gather.11.cloned.1.call-update) | async-done | bytes 16777232 | tf_op jit(solution)/shard_map/all_gather | solution.py:39
  3064.9 14.1 copy.154
  3079.0 8.4 bitcast_reduce_fusion
  3087.4 116.0 %all_gather.35 = f32[256,256]{0,1:T(8,128)S(1)} all-gather(f32[128,256]{0,1:T(8,128)S(1)} %bitcast_reduce_fusion), channel_id=1, replica_groups=mesh['gx_0'=2,'gx_1'=4,'gy'=4,'gz_0'=4,'gz_1'=2] {'gz_1'}, dimensions={0}, use_global_device_ids=true | all-gather | bytes 393216 | tf_op jit(solution)/shard_map/all_gather | solution.py:40
  (391 shorter events, 298.3 us)
Async XLA Ops:
  7.2 19.3 copy-start
  7.2 765.9 %reduce-scatter.6.cloned.1.call-start = ((), (), s32[]{:S(2)}) async-start(), calls=%async_computation.4 | async-start | bytes 393216 | tf_op jit(solution)/shard_map/reduce_scatter | solution.py:38
  7.2 104.3 %collective-permute-start.1 = (f32[1,1,1,3,16,32]{5,4,3,2,1,0:T(8,128)}, f32[1,1,1,3,16,32]{5,4,3,2,1,0:T(8,128)S(1)}, u32[]{:S(2)}, u32[]{:S(2)}) collective-permute-start(f32[1,1,1,3,16,32]{5,4,3,2,1,0:T(8,128)} %bitcast.250), channel_id=1, source_target_pairs={{32,0},{64,32},{96,64},{128,96},{160,128},{192,160},{224,192},{33,... | collective-permute-start | bytes 18440 | tf_op jit(solution)/shard_map/ppermute | solution.py:23
  8.5 103.0 %collective-permute-start = (f32[1,1,1,3,16,32]{5,4,3,2,1,0:T(8,128)}, f32[1,1,1,3,16,32]{5,4,3,2,1,0:T(8,128)S(1)}, u32[]{:S(2)}, u32[]{:S(2)}) collective-permute-start(f32[1,1,1,3,16,32]{5,4,3,2,1,0:T(8,128)} %bitcast.251), channel_id=1, source_target_pairs={{0,32},{32,64},{64,96},{96,128},{128,160},{160,192},{192,224},{1,3... | collective-permute-start | bytes 18440 | tf_op jit(solution)/shard_map/ppermute | solution.py:21
  14.1 355.3 %collective-permute-start.7 = (bf16[1,1,1,32,1536]{4,3,2,1,0:T(8,128)(2,1)S(1)}, bf16[1,1,1,32,1536]{4,3,2,1,0:T(8,128)(2,1)S(1)}, u32[]{:S(2)}, u32[]{:S(2)}) collective-permute-start(bf16[1,1,1,32,1536]{4,3,2,1,0:T(8,128)(2,1)S(1)} %slice.420), channel_id=1, source_target_pairs={{32,0},{64,32},{96,64},{128,96},{160,128},{192,160},{224,192},{33,... | collective-permute-start | bytes 294920 | tf_op jit(solution)/shard_map/ppermute | solution.py:23
  15.4 354.0 %collective-permute-start.6 = (bf16[1,1,1,32,1536]{4,3,2,1,0:T(8,128)(2,1)S(1)}, bf16[1,1,1,32,1536]{4,3,2,1,0:T(8,128)(2,1)S(1)}, u32[]{:S(2)}, u32[]{:S(2)}) collective-permute-start(bf16[1,1,1,32,1536]{4,3,2,1,0:T(8,128)(2,1)S(1)} %slice.420), channel_id=1, source_target_pairs={{0,32},{32,64},{64,96},{96,128},{128,160},{160,192},{192,224},{1,3... | collective-permute-start | bytes 294920 | tf_op jit(solution)/shard_map/ppermute | solution.py:21
  20.7 90.6 %copy-start.2 = (bf16[768,256]{1,0:T(8,128)(2,1)}, bf16[768,256]{1,0:T(8,128)(2,1)S(1)}, u32[]{:S(2)}) copy-start(bf16[768,256]{1,0:T(8,128)(2,1)S(1)} %reshape_squeeze.7) | copy-start | bytes 1179652
  21.8 769.1 %reduce-scatter.4.cloned.1.call-start = ((), (), s32[]{:S(2)}) async-start(), calls=%async_computation.3 | async-start | bytes 393216 | tf_op jit(solution)/shard_map/reduce_scatter | solution.py:38
  26.4 85.1 %copy-start.8 = (f32[1,1,1,3,16,128]{5,4,3,2,1,0:T(8,128)S(1)}, f32[1,1,1,3,16,128]{5,4,3,2,1,0:T(8,128)}, u32[]{:S(2)}) copy-start(f32[1,1,1,3,16,128]{5,4,3,2,1,0:T(8,128)} %param.14) | copy-start | bytes 73732
  111.5 5.3 collective-permute-start.3
  112.8 5.4 collective-permute-start.2
  118.2 11.5 collective-permute-start.5
  124.9 6.0 collective-permute-start.4
  369.4 14.4 copy-start.6
  370.2 13.6 collective-permute-start.9
  371.4 12.3 collective-permute-start.8
  380.4 13.2 copy-start.1
  383.8 14.0 copy-start.5
  385.9 186.9 %collective-permute-start.11 = (bf16[3,3,1,32,1536]{4,3,2,1,0:T(8,128)(2,1)}, bf16[3,3,1,32,1536]{4,3,2,1,0:T(8,128)(2,1)}, u32[]{:S(2)}, u32[]{:S(2)}) collective-permute-start(bf16[3,3,1,32,1536]{4,3,2,1,0:T(8,128)(2,1)} %pad_maximum_fusion.3), channel_id=1, source_target_pairs={{1,0},{2,1},{3,2},{4,3},{5,4},{6,5},{7,6},{9,8},{10,9},{11,10},{12... | collective-permute-start | bytes 2654216 | tf_op jit(solution)/shard_map/ppermute | solution.py:23
  387.8 185.0 %collective-permute-start.10 = (bf16[3,3,1,32,1536]{4,3,2,1,0:T(8,128)(2,1)}, bf16[3,3,1,32,1536]{4,3,2,1,0:T(8,128)(2,1)}, u32[]{:S(2)}, u32[]{:S(2)}) collective-permute-start(bf16[3,3,1,32,1536]{4,3,2,1,0:T(8,128)(2,1)} %pad_maximum_fusion.3), channel_id=1, source_target_pairs={{0,1},{1,2},{2,3},{3,4},{4,5},{5,6},{6,7},{8,9},{9,10},{10,11},{11... | collective-permute-start | bytes 2654216 | tf_op jit(solution)/shard_map/ppermute | solution.py:21
  397.8 175.1 %copy-start.7 = (bf16[1,1,1,32,1536]{4,3,2,1,0:T(8,128)(2,1)S(1)}, bf16[1,1,1,32,1536]{4,3,2,1,0:T(8,128)(2,1)}, u32[]{:S(2)}) copy-start(bf16[1,1,1,32,1536]{4,3,2,1,0:T(8,128)(2,1)} %copy-done.6) | copy-start | bytes 294916
  408.1 166.6 %copy-start.4 = (bf16[1,1,1,128,1536]{4,3,2,1,0:T(8,128)(2,1)S(1)}, bf16[1,1,1,128,1536]{4,3,2,1,0:T(8,128)(2,1)}, u32[]{:S(2)}) copy-start(bf16[1,1,1,128,1536]{4,3,2,1,0:T(8,128)(2,1)} %param.18) | copy-start | bytes 1179652
  764.9 7.0 copy-start.3
  771.9 36.4 %reduce-scatter.8.cloned.1.call-start = ((), (), s32[]{:S(2)}) async-start(), calls=%async_computation.5 | async-start | bytes 393216 | tf_op jit(solution)/shard_map/reduce_scatter | solution.py:38
  773.0 649.2 %all-gather.9.cloned.1.call-start = ((), (), s32[]{:S(2)}) async-start(), calls=%async_computation.7 | async-start | bytes 16908288 | tf_op jit(solution)/shard_map/all_gather | solution.py:39
  773.6 1443.5 %all-gather.7.cloned.1.call-start = ((), (), s32[]{:S(2)}) async-start(), calls=%async_computation.6 | async-start | bytes 16908288 | tf_op jit(solution)/shard_map/all_gather | solution.py:39
  790.9 2274.0 %all-gather.11.cloned.1.call-start = ((), (), s32[]{:S(2)}) async-start(), calls=%async_computation.8 | async-start | bytes 16908288 | tf_op jit(solution)/shard_map/all_gather | solution.py:39
Sparse Core Ops, SparseCore 0:
  21.9 22.0 reduce-scatter.5
  772.0 18.7 reduce-scatter.3
  793.9 14.3 reduce-scatter.7
  809.9 612.2 all-gather.8
  1423.8 793.2 all-gather.6
  2218.7 846.1 all-gather.10
